TPU v7x, 128 devices: a whole 4x4x4 slice. The times are simulated.
128 devices in a mesh: days: 8 (over x, core), fac: 16 (over y, z).
Axes of the slice: x: 4, y: 4, z: 4, core: 2. Of those that a mesh axis runs over, the one named last changes fastest.
Arguments:
- history: bfloat16 [4096, 16384], P('days', 'fac'), may hold values from -1.796875 to 1.796875
- block_starts: int32 [2048, 4], replicated, may hold values from 0 to 4092
- block_lengths: int32 [2048, 4], replicated, may hold values from 1 to 4, 10 in all within a row
- vol_scale: float32 [16384], P('fac'), may hold values from 0.5 to 2
- exposure: bfloat16 [8192, 16384], P('days', 'fac'), may hold values from -0.046875 to 0.046875
- realized: bfloat16 [16384], P('fac'), may hold values from -6 to 6
Outputs:
- path_loss: bfloat16 [8192, 2048], P(('days', 'fac'))
- margin: float32 [8192], P(('days', 'fac'))
- shortfall: float32 [8192], P(('days', 'fac'))
Inputs may be any that keep to these rules, and one draw needn't show every extreme that they name: `block_starts`: every block lies inside the history: a start is at most 4092. `block_lengths`: the 4 lengths of a path sum to 10.
All inputs are finite; a program needn't handle non-finite values.
Results may differ from a plain program's by a relative error of at most 0.019.
Values may be sent and summed in bfloat16 or wider, within the bound.
A program may use at most 64 MiB of HBM per device.

v0:
```python
import jax
import jax.numpy as jnp
from jax import lax
from jax.sharding import PartitionSpec as P


def cut_along(value, dim, size):
    before, after = (value.shape[:dim], value.shape[dim + 1 :])
    return jnp.moveaxis(value.reshape(*before, size, -1, *after), dim, 0)


def sent_and_summed(value, axis, dim):
    size = lax.axis_size(axis)
    blocks = lax.all_to_all(cut_along(value, dim, size), axis, 0, 0, tiled=True)
    return jnp.sum(blocks.astype(jnp.float32), axis=0)


def sent_together(arrays, axis, dim, along):
    columns = [a.reshape(*a.shape[:along], -1) for a in arrays]
    both = jnp.concatenate(columns, axis=along)
    result, at, outs = (sent_and_summed(both, axis, dim), 0, [])
    for a, column in zip(arrays, columns):
        share = result[..., at : at + column.shape[along]]
        outs.append(share.reshape(*share.shape[:along], *a.shape[along:]))
        at += column.shape[along]
    return tuple(outs)


def day_counts(block_starts, block_lengths, count):
    days = lax.broadcasted_iota(jnp.int32, (1, count), 1)
    total = jnp.zeros((block_starts.shape[0], count), jnp.float32)
    for block in range(block_starts.shape[1]):
        lower = block_starts[:, block : block + 1]
        upper = lower + block_lengths[:, block : block + 1]
        total = total + ((days >= lower) & (days < upper)).astype(jnp.float32)
    return total.astype(jnp.bfloat16)


def revalue(exposure, shock_rows):
    return -lax.dot_general(
        exposure, shock_rows, (((1,), (1,)), ((), ())), preferred_element_type=jnp.float32
    )


def local(history, block_starts, block_lengths, vol_scale, exposure, realized):
    piece = lax.all_gather(history, "days", axis=0, tiled=True)
    counts = day_counts(block_starts, block_lengths, piece.shape[0])
    path_sum = jnp.dot(counts, piece, preferred_element_type=jnp.float32)
    shock = (path_sum * vol_scale[None, :]).astype(jnp.bfloat16)
    losses = revalue(exposure, shock)
    realized_part = -jnp.dot(exposure, realized, preferred_element_type=jnp.float32)
    loss_rows, realized_rows = sent_together(
        (losses.astype(jnp.bfloat16), realized_part.astype(jnp.bfloat16)), "fac", 0, 1
    )
    margin = jnp.log(jnp.mean(jnp.exp(loss_rows), axis=1))
    return (loss_rows.astype(jnp.bfloat16), margin, realized_rows - margin)


def solution(mesh):
    in_specs = (P("days", "fac"), P(), P(), P("fac"), P("days", "fac"), P("fac"))
    out_specs = (P(("days", "fac"), None), P(("days", "fac")), P(("days", "fac")))
    return jax.shard_map(local, mesh=mesh, in_specs=in_specs, out_specs=out_specs, check_vma=False)
```

profile of v0, /device:TPU:0, one launch (start us, length us, event | category | flops | bytes accessed | tf_op | source)
XLA Modules:
  0.0 180.3 jit_solution(1145720028164568906)
XLA Ops:
  7.2 0.0 copy-start
  7.2 0.0 all-gather.2.cloned.1.call-start
  7.2 0.7 all-gather.2.cloned.1.call-update
  7.9 0.7 reshape.16
  8.6 0.2 copy-done
  8.8 0.6 fusion.14
  9.4 0.5 concatenate.11
  9.9 1.0 slice_add_fusion.3
  10.9 51.0 %all-gather.2.cloned.1.call-done = bf16[4096,1024]{1,0:T(8,128)(2,1)} async-done(((bf16[512,1024]{1,0:T(8,128)(2,1)}), bf16[4096,1024]{1,0:T(8,128)(2,1)}) %all-gather.2.cloned.1.call-update) | async-done | bytes 8388624 | tf_op jit(solution)/shard_map/all_gather | solution.py:46
  61.9 43.5 %multiply_convert_fusion = bf16[2048,1024]{1,0:T(8,128)(2,1)S(1)} fusion(bf16[4096,1024]{1,0:T(8,128)(2,1)} %all-gather.2.cloned.1.call-done, s32[2048]{0:T(1024)S(1)} %bitcast.21, s32[2048]{0:T(1024)S(1)} %bitcast.25, s32[2048]{0:T(1024)S(1)} %bitcast.22, s32[2048]{0:T(1024)S(1)} %bitcast.26, s32[2048]{0:T(1024)S(1)} %bitcast.20, s32[2048]{0:T(1024)S(1)} %bitcast.24, ...), kind=kOutput, calls=%fused_computation.24 | convolution fusion | flops 17351835648 | bytes 12652544 | tf_op jit(solution)/shard_map/dot_general | solution.py:48
  105.4 4.8 %negate_convert_fusion = bf16[2048,1024]{0,1:T(8,128)(2,1)S(1)} fusion(bf16[2048,1024]{1,0:T(8,128)(2,1)S(1)} %multiply_convert_fusion, bf16[1024,1024]{1,0:T(8,128)(2,1)S(1)} %copy-done), kind=kOutput, calls=%fused_computation.23 | convolution fusion | flops 4299161600 | bytes 10485760 | tf_op jit(solution)/shard_map/dot_general | solution.py:40
  110.2 0.4 pad_maximum_fusion
  110.7 60.7 %all_to_all.5 = bf16[16,64,2049]{2,1,0:T(8,128)(2,1)S(1)} all-to-all(bf16[16,64,2049]{2,1,0:T(8,128)(2,1)S(1)} %pad_maximum_fusion), channel_id=1, replica_groups=mesh['days'=8,'fac'=16] {'fac'}, dimensions={0} | all-to-all | bytes 8392704 | tf_op jit(solution)/shard_map/all_to_all | solution.py:14
  171.3 0.6 convert_reduce_fusion
  171.9 0.2 exponential_reduce_fusion
  172.1 0.1 slice_reduce_fusion
  172.2 0.7 slice.53
  173.0 0.5 fusion.13
  (1 shorter events, 0.0 us)
Async XLA Ops:
  7.2 1.6 copy-start
  7.2 54.7 %all-gather.2.cloned.1.call-start = ((), (), s32[]{:S(2)}) async-start(), calls=%async_computation.1 | async-start | bytes 9437184 | tf_op jit(solution)/shard_map/all_gather | solution.py:46
Sparse Core Ops, SparseCore 0:
  9.7 52.1 all-gather.1
where the time goes:
time: 181 us; the launch traced here: 180 us
  blocking collectives  60.7 us (34%)
  waiting for transfers between devices  51.7 us (29%)
  matrix products  48.9 us (27%)
  between operations  14.1 us (8%)
  other arithmetic  2.77 us (2%)
  local copies, waits for them, and re-layouts  2.16 us (1%)
    all_to_all x1, blocking collectives, sent_and_summed(): blocks = lax.all_to_all(cut_along(value, dim, size), axis, 0, 0, tiled=True)  60.7 us
    all_gather x1, waiting for transfers between devices, local(): piece = lax.all_gather(history, 'days', axis=0, tiled=True)  51 us
    dot_general x1, matrix products, local(): path_sum = jnp.dot(counts, piece, preferred_element_type=jnp.float32)  43.5 us
    dot_general x1, matrix products, revalue(): lax.dot_general(exposure, shock_rows, (((1,), (1,)), ((), ())), preferred...  4.78 us
  transfers between devices with their start and end apart: 1, of which 1 were waited for; matrix products, arithmetic and copies ran while one was open for 2% of the time, Pallas kernels for 0%

commit v1 on v0

v1 whole, which is shorter than its diff:
```python
import functools

import jax
import jax.numpy as jnp
from jax import lax
from jax.experimental import pallas as pl
from jax.experimental.pallas import tpu as pltpu
from jax.sharding import PartitionSpec as P

CHUNKS = 8
STEPS = 4
ORDERS = (
    ("zu", "yu", "zv", "yv"),
    ("zv", "yv", "zu", "yu"),
    ("yu", "zu", "yv", "zv"),
    ("yv", "zv", "yu", "zu"),
)


def bits(place):
    return (place % 2 + place // 2) % 2, place // 2


def slot_of(order, fac):
    yu, yv = bits(fac // 4)
    zu, zv = bits(fac % 4)
    value = {"yu": yu, "yv": yv, "zu": zu, "zv": zv}
    slot = 0
    for name in order:
        slot = slot * 2 + value[name]
    return slot


def remote(src, dst, send, recv, device):
    return pltpu.make_async_remote_copy(
        src_ref=src,
        dst_ref=dst,
        send_sem=send,
        recv_sem=recv,
        device_id=device,
        device_id_type=pl.DeviceIdType.MESH,
    )


def kernel(
    hist, starts, lens, vol, expo, real,
    out, margin, shortfall,
    days, book, counts, part, part_in, pair, pair_in, shock,
    loss0, loss1, loss2, loss3, in0, in1, in2, in3, sums, owed,
    here, days_send, days_recv, x_send, x_recv, sib_send, sib_recv, f_send, f_recv,
):
    own_days, width = hist.shape
    paths = starts.shape[1]
    d = lax.axis_index("days")
    f = lax.axis_index("fac")
    x, c = d // 2, d % 2
    y, z = f // 4, f % 4
    u, v = bits(x)
    yu, yv = bits(y)
    zu, zv = bits(z)
    sibling = {"days": x * 2 + 1 - c}
    over_u = {"days": (x + 1 - 2 * (x % 2)) * 2 + c}
    over_v = {"days": (3 - x) * 2 + c}
    place = {"yu": yu, "yv": yv, "zu": zu, "zv": zv}
    partner = {
        "zu": {"fac": y * 4 + z + 1 - 2 * (z % 2)},
        "zv": {"fac": y * 4 + 3 - z},
        "yu": {"fac": (y + 1 - 2 * (y % 2)) * 4 + z},
        "yv": {"fac": (3 - y) * 4 + z},
    }
    first, second = (u, v), (v, u)
    over_first, over_second = (over_u, over_v), (over_v, over_u)
    losses, arrivals = (loss0, loss1, loss2, loss3), (in0, in1, in2, in3)

    load_book = pltpu.make_async_copy(expo, book, here.at[0])
    load_days = pltpu.make_async_copy(hist, days.at[c], here.at[1])
    load_days.start()
    load_book.start()
    barrier = pltpu.get_barrier_semaphore()
    everyone = (sibling, over_u, over_v, *partner.values())
    for device in everyone:
        pl.semaphore_signal(barrier, inc=1, device_id=device, device_id_type=pl.DeviceIdType.MESH)
    pl.semaphore_wait(barrier, len(everyone))

    share_days = remote(hist, days.at[c], days_send, days_recv, sibling)
    share_days.start()

    shock[0] = jnp.zeros(shock.shape[1:], shock.dtype)
    rows = lax.broadcasted_iota(jnp.int32, (16, width), 0)
    moved = jnp.broadcast_to(-real[...].astype(jnp.float32), (16, width))
    shock[0, 0, 0, 0, 0] = jnp.where(rows == 0, moved, 0.0).astype(shock.dtype)
    sums[...] = jnp.zeros_like(sums)

    half = paths // CHUNKS // 2
    chip_days = 2 * own_days

    def count_days(q, carry):
        at = pl.multiple_of((q * 2 + c) * half, half)
        low = starts[:, pl.ds(at, half)]
        both = jnp.concatenate([low, low + lens[:, pl.ds(at, half)]], axis=0).astype(jnp.float32)
        table = jnp.concatenate([both] * (half // 8), axis=0).T
        day = (lax.broadcasted_iota(jnp.int32, (16, chip_days), 1) + x * chip_days).astype(jnp.float32)
        for group in range(half // 16):
            piece = table[group * 16 : group * 16 + 16]
            total = jnp.zeros((16, chip_days), jnp.float32)
            for block in range(4):
                inside = (day >= piece[:, block : block + 1]) & (day < piece[:, block + 4 : block + 5])
                total = total + jnp.where(inside, 1.0, 0.0)
            counts[q, group * 16 : group * 16 + 16, :] = total.astype(counts.dtype)
        return carry

    lax.fori_loop(0, CHUNKS, count_days, 0)
    load_days.wait()
    share_days.wait()
    load_book.wait()

    def scatter_one(q, s):
        return remote(part.at[q, s, 1 - first[s]], part_in.at[q, s], x_send.at[0, s], x_recv.at[0, s, q], over_first[s])

    def scatter_two(q, s):
        return remote(pair.at[q, s, 1 - second[s]], pair_in.at[q, s], x_send.at[1, s], x_recv.at[1, s, q], over_second[s])

    def gather_one(q, s, block):
        rows = shock.at[q + 1, c, s, first[s], block]
        return remote(rows, rows, x_send.at[2, s], x_recv.at[2, s, q], over_second[s])

    def gather_two(q, s, block):
        rows = shock.at[q + 1, c, s, block]
        return remote(rows, rows, x_send.at[3, s], x_recv.at[3, s, q], over_first[s])

    def give_sibling(q, core):
        rows = shock.at[q + 1, core]
        return remote(rows, rows, sib_send, sib_recv.at[q], sibling)

    def pass_losses(step, r, k):
        name = ORDERS[k][step]
        return remote(
            losses[step].at[r, k, 1 - place[name]], arrivals[step].at[r, k],
            f_send.at[step, k], f_recv.at[step, k, r], partner[name],
        )

    def launch(copy, turn):
        @pl.when(turn > 0)
        def _():
            copy.wait_send()
        copy.start()

    def stage(turn, count, body):
        @pl.when((turn >= 0) & (turn < count))
        def _():
            body(turn)

    def sum_days(q):
        whole = days[...].reshape(chip_days, width)
        total = jnp.dot(counts[q], whole, preferred_element_type=jnp.float32).astype(part.dtype)
        part[q] = total.reshape(part.shape[1:])
        for s in range(2):
            launch(scatter_one(q, s), q)

    def sum_pairs(q):
        for s in range(2):
            scatter_one(q, s).wait_recv()
            total = part[q, s, first[s]].astype(jnp.float32) + part_in[q, s].astype(jnp.float32)
            pair[q, s] = total.astype(pair.dtype).reshape(pair.shape[2:])
            launch(scatter_two(q, s), q)

    def sum_chips(q):
        for s in range(2):
            scatter_two(q, s).wait_recv()
            total = pair[q, s, second[s]].astype(jnp.float32) + pair_in[q, s].astype(jnp.float32)
            shock[q + 1, c, s, first[s], second[s]] = (total * -vol[...]).astype(shock.dtype)
            launch(gather_one(q, s, second[s]), q)

    def spread(q):
        for s in range(2):
            gather_one(q, s, 1 - second[s]).wait_recv()
            launch(gather_two(q, s, first[s]), q)

    def cross(q):
        for s in range(2):
            gather_two(q, s, 1 - first[s]).wait_recv()
        launch(give_sibling(q, c), q)

    def revalue(r):
        @pl.when(r > 0)
        def _():
            give_sibling(r - 1, 1 - c).wait_recv()
        moves = shock[r].reshape(2 * half, width)
        value = lax.dot_general(
            book[...], moves, (((1,), (1,)), ((), ())), preferred_element_type=jnp.float32
        ).astype(loss0.dtype)
        span = loss0.shape[3] // 8
        for k in range(4):
            lane, row = k // 2 * 128, k % 2 * span
            for owner in range(16):
                slot = slot_of(ORDERS[k], owner)
                at = slot % 8 * span
                loss0[r, k, slot // 8, at : at + span, :] = value[
                    owner * 2 * span + row : owner * 2 * span + row + span, lane : lane + 128
                ]
            launch(pass_losses(0, r, k), r)

    def fold(step, r):
        for k in range(4):
            pass_losses(step - 1, r, k).wait_recv()
            kept = losses[step - 1][r, k, place[ORDERS[k][step - 1]]]
            total = kept.astype(jnp.float32) + arrivals[step - 1][r, k].astype(jnp.float32)
            losses[step][r, k] = total.astype(loss0.dtype).reshape(losses[step].shape[2:])
            launch(pass_losses(step, r, k), r)

    def finish(r):
        span = in3.shape[2]
        for k in range(4):
            pass_losses(3, r, k).wait_recv()
            kept = loss3[r, k, place[ORDERS[k][3]]]
            loss = kept.astype(jnp.float32) + in3[r, k].astype(jnp.float32)
            lane, row = k // 2 * 128, k % 2 * span

            @pl.when(r > 0)
            def _():
                at = pl.multiple_of((r - 1) * 2 * half + lane, 128)
                out[row : row + span, pl.ds(at, 128)] = loss.astype(out.dtype)
                sums[row : row + span, :] = sums[row : row + span, :] + jnp.exp(loss)

            if lane == 0:

                @pl.when(r == 0)
                def _():
                    owed[row : row + span, :] = loss

    def turn(t, carry):
        stage(t - 1, CHUNKS, sum_pairs)
        stage(t - 2, CHUNKS, sum_chips)
        stage(t - 3, CHUNKS, spread)
        stage(t - 4, CHUNKS, cross)
        stage(t, CHUNKS, sum_days)
        stage(t - 4, CHUNKS + 1, revalue)
        for step in range(1, 4):
            stage(t - 4 - step, CHUNKS + 1, functools.partial(fold, step))
        stage(t - 8, CHUNKS + 1, finish)
        return carry

    lax.fori_loop(0, CHUNKS + 9, turn, 0)

    last = CHUNKS - 1
    for s in range(2):
        scatter_one(last, s).wait_send()
        scatter_two(last, s).wait_send()
        gather_one(last, s, second[s]).wait_send()
        gather_two(last, s, first[s]).wait_send()
    give_sibling(last, c).wait_send()
    for k in range(4):
        for step in range(4):
            pass_losses(step, CHUNKS, k).wait_send()

    count = out.shape[0]
    level = jnp.log(jnp.sum(sums[...], axis=1, keepdims=True) * (1.0 / paths))
    diagonal = lax.broadcasted_iota(jnp.int32, (count, count), 0) == lax.broadcasted_iota(
        jnp.int32, (count, count), 1
    )
    margin[...] = jnp.sum(jnp.where(diagonal, level, 0.0), axis=0, keepdims=True)
    over = owed[:, 0:1] - level
    shortfall[...] = jnp.sum(jnp.where(diagonal, over, 0.0), axis=0, keepdims=True)


def local(history, block_starts, block_lengths, vol_scale, exposure, realized):
    own_days, width = history.shape
    paths = block_starts.shape[0]
    accounts = exposure.shape[0]
    mine = accounts // 16
    q, r = CHUNKS, CHUNKS + 1
    half = paths // q // 2
    block = half // 8
    whole = functools.partial(pl.BlockSpec, memory_space=pltpu.VMEM)
    raw = pl.BlockSpec(memory_space=pl.ANY)
    bf16, f32 = jnp.bfloat16, jnp.float32
    quarter = mine // 2
    dma = pltpu.SemaphoreType.DMA
    out, margin, shortfall = pl.pallas_call(
        kernel,
        out_shape=(
            jax.ShapeDtypeStruct((mine, paths), bf16),
            jax.ShapeDtypeStruct((1, mine), f32),
            jax.ShapeDtypeStruct((1, mine), f32),
        ),
        in_specs=[raw, whole(), whole(), whole(), raw, whole()],
        out_specs=(whole(), whole(), whole()),
        scratch_shapes=[
            pltpu.VMEM((2, own_days, width), bf16),
            pltpu.VMEM((accounts, width), bf16),
            pltpu.VMEM((q, half, 2 * own_days), bf16),
            pltpu.VMEM((q, 2, 2, 2 * block, width), bf16),
            pltpu.VMEM((q, 2, 2 * block, width), bf16),
            pltpu.VMEM((q, 2, 2, block, width), bf16),
            pltpu.VMEM((q, 2, block, width), bf16),
            pltpu.VMEM((r, 2, 2, 2, 2, block, width), bf16),
            *[pltpu.VMEM((r, 4, 2, (8 >> step) * quarter, 128), bf16) for step in range(4)],
            *[pltpu.VMEM((r, 4, (8 >> step) * quarter, 128), bf16) for step in range(4)],
            pltpu.VMEM((mine, 128), f32),
            pltpu.VMEM((mine, 128), f32),
            dma((2,)),
            dma,
            dma,
            dma((4, 2)),
            dma((4, 2, q)),
            dma,
            dma((q,)),
            dma((4, 4)),
            dma((4, 4, r)),
        ],
        compiler_params=pltpu.CompilerParams(
            collective_id=0, has_side_effects=True, vmem_limit_bytes=56 << 20
        ),
        name="backtest",
    )(
        history,
        block_starts.T,
        block_lengths.T,
        vol_scale.reshape(1, width),
        exposure,
        realized.reshape(1, width),
    )
    return out, margin.reshape(mine), shortfall.reshape(mine)


def solution(mesh):
    in_specs = (P("days", "fac"), P(), P(), P("fac"), P("days", "fac"), P("fac"))
    out_specs = (P(("days", "fac"), None), P(("days", "fac")), P(("days", "fac")))
    return jax.shard_map(local, mesh=mesh, in_specs=in_specs, out_specs=out_specs, check_vma=False)
```

time: 181 us -> 94.5 us (0.52)
  Pallas kernels: 0 us -> 88.5 us
  blocking collectives: 60.7 us -> 0 us
  waiting for transfers between devices: 51.7 us -> 0 us
  matrix products: 48.9 us -> 0 us
  between operations: 14.1 us -> 0.64 us
  local copies, waits for them, and re-layouts: 2.16 us -> 5.16 us
  other arithmetic: 2.77 us -> 0 us
    pallas_call x0 -> x1, Pallas kernels: none -> 88.5 us  [local(): pl.pallas_call(kernel, out_shape=(jax.ShapeDtypeStruct((mine, paths), bf1...]
    all_to_all x1 -> x0, blocking collectives: 60.7 us -> none  [sent_and_summed(): blocks = lax.all_to_all(cut_along(value, dim, size), axis, 0, 0, tiled=True)]
    all_gather x1 -> x0, waiting for transfers between devices: 51 us -> none  [local(): piece = lax.all_gather(history, 'days', axis=0, tiled=True)]
    dot_general x3 -> x0, matrix products: 48.9 us -> none  [the longest x1 43.5 us: local(): path_sum = jnp.dot(counts, piece, preferred_element_type=jnp.float32)]
    unnamed x3, local copies, waits for them, and re-layouts: 0.85 us -> 3.88 us
  transfers between devices with their start and end apart: 1 -> 0, of which waited for: 1 -> 0; matrix products, arithmetic and copies ran while one was open for 2% -> 0% of each run, Pallas kernels for 0% -> 0%
where the time goes in v1:
time: 94.5 us; the launch traced here: 94.3 us
  Pallas kernels  88.5 us (94%)
  local copies, waits for them, and re-layouts  5.16 us (5%)
    pallas_call x1, Pallas kernels, local(): pl.pallas_call(kernel, out_shape=(jax.ShapeDtypeStruct((mine, paths), bf1...  88.5 us
    unnamed x3, local copies, waits for them, and re-layouts  3.88 us

profile of v1, /device:TPU:0, one launch (start us, length us, event | category | flops | bytes accessed | tf_op | source)
XLA Modules:
  0.0 94.3 jit_solution(6602112957057690991)
XLA Ops:
  0.6 1.3 %reshape.19.real = bf16[1,1024]{1,0:T(2,128)(2,1)} reshape(bf16[1024]{0:T(1024)(128)(2,1)} %param.11) | data formatting | bytes 4096 | tf_op jit(solution)/shard_map/reshape | solution.py:321
  1.9 88.5 %backtest.1 = (bf16[64,2048]{1,0:T(8,128)(2,1)}, f32[1,64]{1,0:T(1,128)}, f32[1,64]{1,0:T(1,128)}) custom-call(bf16[512,1024]{1,0:T(8,128)(2,1)} %hist.1, s32[4,2048]{1,0:T(4,128)} %bitcast.5, s32[4,2048]{1,0:T(4,128)} %bitcast.6, f32[1,1024]{1,0:T(1,128)} %bitcast.7, bf16[1024,1024]{1,0:T(8,128)(2,1)} %expo.1, bf16[1,1024]{1,0:T(2,128)(2,1)} %reshape.19.real), custom_call_target="tpu_custom_call" | custom-call | tf_op jit(solution)/shard_map/backtest/pallas_call | solution.py:279
  90.4 1.7 %copy.12 = bf16[64,2048]{1,0:T(8,128)(2,1)} copy(bf16[64,2048]{1,0:T(8,128)(2,1)} %get-tuple-element.12) | data formatting | bytes 524288
  92.0 1.1 %copy.13 = f32[64]{0:T(128)} copy(f32[64]{0:T(128)} %bitcast.9) | data formatting | bytes 512
  93.2 1.1 %copy.14 = f32[64]{0:T(128)} copy(f32[64]{0:T(128)} %bitcast.8) | data formatting | bytes 512

commit v2 on v1

v2 whole, which is shorter than its diff:
```python
import functools

import jax
import jax.numpy as jnp
from jax import lax
from jax.experimental import pallas as pl
from jax.experimental.pallas import tpu as pltpu
from jax.sharding import PartitionSpec as P

CHUNKS = 8
PAIRS, CHIPS, SPREAD, CROSS, REVALUE, FOLD, FINISH = 2, 3, 4, 5, 5, 6, 7


def bits(place):
    return (place % 2 + place // 2) % 2, place // 2


def remote(src, dst, send, recv, device):
    return pltpu.make_async_remote_copy(
        src_ref=src,
        dst_ref=dst,
        send_sem=send,
        recv_sem=recv,
        device_id=device,
        device_id_type=pl.DeviceIdType.MESH,
    )


def kernel(
    hist, starts, lens, vol, expo, real,
    out, margin, shortfall,
    days, book, counts, part, part_in, pair, pair_in, shock,
    loss, loss_in, row, row_in, sums, owed,
    here, days_send, days_recv, x_send, x_recv, sib_send, sib_recv, f_send, f_recv,
):
    own_days, width = hist.shape
    paths = starts.shape[1]
    d = lax.axis_index("days")
    f = lax.axis_index("fac")
    x, c = d // 2, d % 2
    y, z = f // 4, f % 4
    u, v = bits(x)
    sibling = {"days": x * 2 + 1 - c}
    over_u = {"days": (x + 1 - 2 * (x % 2)) * 2 + c}
    over_v = {"days": (3 - x) * 2 + c}
    over_y = [{"fac": (y + j) % 4 * 4 + z} for j in range(1, 4)]
    over_z = [{"fac": y * 4 + (z + j) % 4} for j in range(1, 4)]
    first, second = (u, v), (v, u)
    over_first, over_second = (over_u, over_v), (over_v, over_u)
    place = ((z, y), (y, z))
    over_place = ((over_z, over_y), (over_y, over_z))

    load_book = pltpu.make_async_copy(expo, book, here.at[0])
    load_days = pltpu.make_async_copy(hist, days.at[c], here.at[1])
    load_days.start()
    load_book.start()
    barrier = pltpu.get_barrier_semaphore()
    everyone = (sibling, over_u, over_v, *over_y, *over_z)
    for device in everyone:
        pl.semaphore_signal(barrier, inc=1, device_id=device, device_id_type=pl.DeviceIdType.MESH)
    pl.semaphore_wait(barrier, len(everyone))

    share_days = remote(hist, days.at[c], days_send, days_recv, sibling)
    share_days.start()

    shock[0] = jnp.zeros(shock.shape[1:], shock.dtype)
    lead = shock.shape[5]
    rows = lax.broadcasted_iota(jnp.int32, (lead, width), 0)
    moved = jnp.broadcast_to(-real[...].astype(jnp.float32).reshape(1, width), (lead, width))
    shock[0, 0, 0, 0, 0] = jnp.where(rows == 0, moved, 0.0).astype(shock.dtype)
    sums[...] = jnp.zeros_like(sums)

    half = paths // CHUNKS // 2
    chip_days = 2 * own_days
    mine = out.shape[0]

    def count_days(q):
        at = pl.multiple_of((q * 2 + c) * half, half)
        low = starts[:, pl.ds(at, half)]
        both = jnp.concatenate([low, low + lens[:, pl.ds(at, half)]], axis=0).astype(jnp.float32)
        table = jnp.concatenate([both] * (half // 8), axis=0).T
        day = (lax.broadcasted_iota(jnp.int32, (16, chip_days), 1) + x * chip_days).astype(jnp.float32)
        for group in range(half // 16):
            piece = table[group * 16 : group * 16 + 16]
            total = jnp.zeros((16, chip_days), jnp.float32)
            for block in range(4):
                inside = (day >= piece[:, block : block + 1]) & (day < piece[:, block + 4 : block + 5])
                total = total + jnp.where(inside, 1.0, 0.0)
            counts[q, group * 16 : group * 16 + 16, :] = total.astype(counts.dtype)

    count_days(0)
    load_days.wait()
    share_days.wait()

    def scatter_one(q, s):
        return remote(part.at[q, s, 1 - first[s]], part_in.at[q, s], x_send.at[0, s, q], x_recv.at[0, s, q], over_first[s])

    def scatter_two(q, s):
        return remote(pair.at[q, s, 1 - second[s]], pair_in.at[q, s], x_send.at[1, s, q], x_recv.at[1, s, q], over_second[s])

    def gather_one(q, s, block):
        rows = shock.at[q + 1, c, s, first[s], block]
        return remote(rows, rows, x_send.at[2, s, q], x_recv.at[2, s, q], over_second[s])

    def gather_two(q, s, block):
        rows = shock.at[q + 1, c, s, block]
        return remote(rows, rows, x_send.at[3, s, q], x_recv.at[3, s, q], over_first[s])

    def give_sibling(q, core):
        rows = shock.at[q + 1, core]
        return remote(rows, rows, sib_send.at[q], sib_recv.at[q], sibling)

    def pass_loss(r, h, j):
        return remote(
            loss.at[r, h, (place[h][0] + j) % 4], loss_in.at[r, h, j - 1],
            f_send.at[0, h, j - 1, r], f_recv.at[0, h, j - 1, r], over_place[h][0][j - 1],
        )

    def pass_row(r, h, j):
        return remote(
            row.at[r, h, (place[h][1] + j) % 4], row_in.at[r, h, j - 1],
            f_send.at[1, h, j - 1, r], f_recv.at[1, h, j - 1, r], over_place[h][1][j - 1],
        )

    def stage(turn, count, body):
        @pl.when((turn >= 0) & (turn < count))
        def _():
            body(turn)

    def sum_days(q):
        whole = days[...].reshape(chip_days, width)
        total = jnp.dot(counts[q], whole, preferred_element_type=jnp.float32).astype(part.dtype)
        part[q] = total.reshape(part.shape[1:])
        for s in range(2):
            scatter_one(q, s).start()

    def sum_pairs(q):
        for s in range(2):
            scatter_one(q, s).wait_recv()
            total = part[q, s, first[s]].astype(jnp.float32) + part_in[q, s].astype(jnp.float32)
            pair[q, s] = total.astype(pair.dtype).reshape(pair.shape[2:])
            scatter_two(q, s).start()

    def sum_chips(q):
        for s in range(2):
            scatter_two(q, s).wait_recv()
            total = pair[q, s, second[s]].astype(jnp.float32) + pair_in[q, s].astype(jnp.float32)
            shock[q + 1, c, s, first[s], second[s]] = (total * -vol[...]).astype(shock.dtype)
            gather_one(q, s, second[s]).start()

    def spread(q):
        for s in range(2):
            gather_one(q, s, 1 - second[s]).wait_recv()
            gather_two(q, s, first[s]).start()

    def cross(q):
        for s in range(2):
            gather_two(q, s, 1 - first[s]).wait_recv()
        give_sibling(q, c).start()

    def revalue(r):
        @pl.when(r == 0)
        def _():
            load_book.wait()

        @pl.when(r > 0)
        def _():
            give_sibling(r - 1, 1 - c).wait_recv()

        moves = shock[r].reshape(2 * half, width)
        value = lax.dot_general(
            book[...], moves, (((1,), (1,)), ((), ())), preferred_element_type=jnp.float32
        ).astype(loss.dtype)
        for h in range(2):
            for owner in range(16):
                at = (owner // 4, owner % 4) if h else (owner % 4, owner // 4)
                loss[r, h, at[0], at[1]] = value[owner * mine : owner * mine + mine, h * half : h * half + half]
            for j in range(1, 4):
                pass_loss(r, h, j).start()

    def fold(r):
        for h in range(2):
            total = loss[r, h, place[h][0]].astype(jnp.float32)
            for j in range(1, 4):
                pass_loss(r, h, j).wait_recv()
                total = total + loss_in[r, h, j - 1].astype(jnp.float32)
            row[r, h] = total.astype(row.dtype)
            for j in range(1, 4):
                pass_row(r, h, j).start()

    def finish(r):
        for h in range(2):
            total = row[r, h, place[h][1]].astype(jnp.float32)
            for j in range(1, 4):
                pass_row(r, h, j).wait_recv()
                total = total + row_in[r, h, j - 1].astype(jnp.float32)

            @pl.when(r > 0)
            def _():
                at = pl.multiple_of(((r - 1) * 2 + h) * half, half)
                out[:, pl.ds(at, half)] = total.astype(out.dtype)
                sums[...] = sums[...] + jnp.exp(total)

            if h == 0:

                @pl.when(r == 0)
                def _():
                    owed[...] = total

    def turn(t, carry):
        stage(t - PAIRS, CHUNKS, sum_pairs)
        stage(t - CHIPS, CHUNKS, sum_chips)
        stage(t - SPREAD, CHUNKS, spread)
        stage(t - CROSS, CHUNKS, cross)
        stage(t, CHUNKS, sum_days)
        stage(t + 1, CHUNKS, count_days)
        stage(t - REVALUE, CHUNKS + 1, revalue)
        stage(t - FOLD, CHUNKS + 1, fold)
        stage(t - FINISH, CHUNKS + 1, finish)
        return carry

    lax.fori_loop(0, CHUNKS + 1 + FINISH, turn, 0)

    level = jnp.log(jnp.sum(sums[...], axis=1, keepdims=True) * (1.0 / paths))
    diagonal = lax.broadcasted_iota(jnp.int32, (mine, mine), 0) == lax.broadcasted_iota(
        jnp.int32, (mine, mine), 1
    )
    margin[...] = jnp.sum(jnp.where(diagonal, level, 0.0), axis=0, keepdims=True)
    over = owed[:, 0:1] - level
    shortfall[...] = jnp.sum(jnp.where(diagonal, over, 0.0), axis=0, keepdims=True)

    def sent(r, carry):
        for h in range(2):
            for j in range(1, 4):
                pass_loss(r, h, j).wait_send()
                pass_row(r, h, j).wait_send()

        @pl.when(r < CHUNKS)
        def _():
            for s in range(2):
                scatter_one(r, s).wait_send()
                scatter_two(r, s).wait_send()
                gather_one(r, s, second[s]).wait_send()
                gather_two(r, s, first[s]).wait_send()
            give_sibling(r, c).wait_send()

        return carry

    lax.fori_loop(0, CHUNKS + 1, sent, 0)


def hand_over(*refs):
    for array, result in zip(refs[:3], refs[3:]):
        result[...] = array[...]


def local(history, block_starts, block_lengths, vol_scale, exposure, realized):
    own_days, width = history.shape
    paths = block_starts.shape[0]
    accounts = exposure.shape[0]
    mine = accounts // 16
    q, r = CHUNKS, CHUNKS + 1
    half = paths // q // 2
    block = half // 8
    vmem = pl.BlockSpec(memory_space=pltpu.VMEM)
    raw = pl.BlockSpec(memory_space=pl.ANY)
    bf16, f32 = jnp.bfloat16, jnp.float32
    dma = pltpu.SemaphoreType.DMA
    results = (
        jax.ShapeDtypeStruct((mine, paths), bf16),
        jax.ShapeDtypeStruct((1, mine), f32),
        jax.ShapeDtypeStruct((1, mine), f32),
    )
    found = pl.pallas_call(
        kernel,
        out_shape=results,
        in_specs=[raw, vmem, vmem, vmem, raw, vmem],
        out_specs=(vmem, vmem, vmem),
        scratch_shapes=[
            pltpu.VMEM((2, own_days, width), bf16),
            pltpu.VMEM((accounts, width), bf16),
            pltpu.VMEM((q, half, 2 * own_days), bf16),
            pltpu.VMEM((q, 2, 2, 2 * block, width), bf16),
            pltpu.VMEM((q, 2, 2 * block, width), bf16),
            pltpu.VMEM((q, 2, 2, block, width), bf16),
            pltpu.VMEM((q, 2, block, width), bf16),
            pltpu.VMEM((r, 2, 2, 2, 2, block, width), bf16),
            pltpu.VMEM((r, 2, 4, 4, mine, half), bf16),
            pltpu.VMEM((r, 2, 3, 4, mine, half), bf16),
            pltpu.VMEM((r, 2, 4, mine, half), bf16),
            pltpu.VMEM((r, 2, 3, mine, half), bf16),
            pltpu.VMEM((mine, half), f32),
            pltpu.VMEM((mine, half), f32),
            dma((2,)),
            dma,
            dma,
            dma((4, 2, q)),
            dma((4, 2, q)),
            dma((q,)),
            dma((q,)),
            dma((2, 2, 3, r)),
            dma((2, 2, 3, r)),
        ],
        compiler_params=pltpu.CompilerParams(
            collective_id=0, has_side_effects=True, vmem_limit_bytes=60 << 20
        ),
        name="backtest",
    )(history, block_starts.T, block_lengths.T, vol_scale.reshape(1, width), exposure, realized)
    out, margin, shortfall = pl.pallas_call(
        hand_over,
        out_shape=results,
        in_specs=[vmem] * 3,
        out_specs=(vmem,) * 3,
        name="results",
    )(*found)
    return out, margin.reshape(mine), shortfall.reshape(mine)


def solution(mesh):
    in_specs = (P("days", "fac"), P(), P(), P("fac"), P("days", "fac"), P("fac"))
    out_specs = (P(("days", "fac"), None), P(("days", "fac")), P(("days", "fac")))
    return jax.shard_map(local, mesh=mesh, in_specs=in_specs, out_specs=out_specs, check_vma=False)
```

time: 94.5 us -> 75.2 us (0.80)
  Pallas kernels: 88.5 us -> 74.4 us
  local copies, waits for them, and re-layouts: 5.16 us -> 0 us
    pallas_call x1 -> x2, Pallas kernels: 88.5 us -> 74.4 us  [the longest x1 72.7 us: local(): pl.pallas_call(kernel, out_shape=results, in_specs=[raw, vmem, vmem, vmem...]
    unnamed x3 -> x0, local copies, waits for them, and re-layouts: 3.88 us -> none
    reshape x1 -> x0, local copies, waits for them, and re-layouts: 1.28 us -> none  [local(): realized.reshape(1, width)]
where the time goes in v2:
time: 75.2 us; the launch traced here: 75 us
  Pallas kernels  74.4 us (99%)
    pallas_call x1, Pallas kernels, local(): pl.pallas_call(kernel, out_shape=results, in_specs=[raw, vmem, vmem, vmem...  72.7 us
    pallas_call x1, Pallas kernels, local(): pl.pallas_call(hand_over, out_shape=results, in_specs=[vmem] * 3, out_spe...  1.68 us

profile of v2, /device:TPU:0, one launch (start us, length us, event | category | flops | bytes accessed | tf_op | source)
XLA Modules:
  0.0 75.0 jit_solution(15747277886378190478)
XLA Ops:
  0.6 72.7 %backtest.1 = (bf16[64,2048]{1,0:T(8,128)(2,1)}, f32[1,64]{1,0:T(1,128)}, f32[1,64]{1,0:T(1,128)}) custom-call(bf16[512,1024]{1,0:T(8,128)(2,1)} %hist.1, s32[4,2048]{1,0:T(4,128)} %bitcast.5, s32[4,2048]{1,0:T(4,128)} %bitcast.6, f32[1,1024]{1,0:T(1,128)} %bitcast.7, bf16[1024,1024]{1,0:T(8,128)(2,1)} %expo.1, bf16[1024]{0:T(1024)(128)(2,1)} %real.1), custom_call_target="tpu_custom_call" | custom-call | tf_op jit(solution)/shard_map/backtest/pallas_call | solution.py:274
  73.3 1.7 %results.1 = (bf16[64,2048]{1,0:T(8,128)(2,1)}, f32[1,64]{1,0:T(1,128)}, f32[1,64]{1,0:T(1,128)}) custom-call(bf16[64,2048]{1,0:T(8,128)(2,1)} %get-tuple-element.9.refs_0_, f32[1,64]{1,0:T(1,128)} %get-tuple-element.10.refs_1_, f32[1,64]{1,0:T(1,128)} %get-tuple-element.11.refs_2_), custom_call_target="tpu_custom_call" | custom-call | tf_op jit(solution)/shard_map/results/pallas_call | solution.py:309

commit v3 on v2

v3 whole, which is shorter than its diff:
```python
import functools

import jax
import jax.numpy as jnp
from jax import lax
from jax.experimental import pallas as pl
from jax.experimental.pallas import tpu as pltpu
from jax.sharding import PartitionSpec as P

CHUNKS = 16
PAIRS, CHIPS, SPREAD, CROSS, REVALUE, FOLD, FINISH = 3, 5, 7, 9, 9, 12, 14
DEEP = 4


def bits(place):
    return (place % 2 + place // 2) % 2, place // 2


def remote(src, dst, send, recv, device):
    return pltpu.make_async_remote_copy(
        src_ref=src,
        dst_ref=dst,
        send_sem=send,
        recv_sem=recv,
        device_id=device,
        device_id_type=pl.DeviceIdType.MESH,
    )


def kernel(
    hist, starts, lens, vol, expo, real,
    out, margin, shortfall,
    days, book, table, counts, part, part_in, pair, pair_in, shock,
    loss, loss_in, row, row_in, sums, owed,
    here, days_send, days_recv, x_send, x_recv, sib_send, sib_recv, f_send, f_recv,
):
    own_days, width = hist.shape
    paths = starts.shape[1]
    d = lax.axis_index("days")
    f = lax.axis_index("fac")
    x, c = d // 2, d % 2
    y, z = f // 4, f % 4
    u, v = bits(x)
    sibling = {"days": x * 2 + 1 - c}
    over_u = {"days": (x + 1 - 2 * (x % 2)) * 2 + c}
    over_v = {"days": (3 - x) * 2 + c}
    over_y = [{"fac": (y + j) % 4 * 4 + z} for j in range(1, 4)]
    over_z = [{"fac": y * 4 + (z + j) % 4} for j in range(1, 4)]
    first, second = (u, v), (v, u)
    over_first, over_second = (over_u, over_v), (over_v, over_u)
    place = ((z, y), (y, z))
    over_place = ((over_z, over_y), (over_y, over_z))

    load_book = pltpu.make_async_copy(expo, book, here.at[0])
    load_days = pltpu.make_async_copy(hist, days.at[c], here.at[1])
    load_days.start()
    load_book.start()
    barrier = pltpu.get_barrier_semaphore()
    everyone = (sibling, over_u, over_v, *over_y, *over_z)
    for device in everyone:
        pl.semaphore_signal(barrier, inc=1, device_id=device, device_id_type=pl.DeviceIdType.MESH)
    pl.semaphore_wait(barrier, len(everyone))

    share_days = remote(hist, days.at[c], days_send, days_recv, sibling)
    share_days.start()

    shock[0] = jnp.zeros(shock.shape[1:], shock.dtype)
    lead = shock.shape[4]
    rows = lax.broadcasted_iota(jnp.int32, (lead, width), 0)
    moved = jnp.broadcast_to(-real[...].astype(jnp.float32).reshape(1, width), (lead, width))
    shock[0, 0, 0, 0] = jnp.where(rows == 0, moved, 0.0).astype(shock.dtype)
    sums[...] = jnp.zeros_like(sums)

    half = paths // CHUNKS // 2
    wide = width // 2
    chip_days = 2 * own_days
    mine = out.shape[0]

    def count_days(q):
        at = (q * 2 + c) * half
        lanes = pl.ds(pl.multiple_of(at // 128 * 128, 128), 128)
        low = starts[:, lanes]
        both = jnp.concatenate([low, low + lens[:, lanes]], axis=0).astype(jnp.float32)
        table[...] = jnp.concatenate([both] * 16, axis=0).T
        day = (lax.broadcasted_iota(jnp.int32, (16, chip_days), 1) + x * chip_days).astype(jnp.float32)
        for group in range(half // 16):
            piece = table[pl.ds(pl.multiple_of(at % 128 + group * 16, 16), 16), :]
            total = jnp.zeros((16, chip_days), jnp.float32)
            for block in range(4):
                inside = (day >= piece[:, block : block + 1]) & (day < piece[:, block + 4 : block + 5])
                total = total + jnp.where(inside, 1.0, 0.0)
            counts[q, group * 16 : group * 16 + 16, :] = total.astype(counts.dtype)

    count_days(0)
    count_days(1)
    load_days.wait()
    share_days.wait()

    def scatter_one(q, s):
        theirs = part.at[q, 1, :, 1 - v] if s else part.at[q, 0, 1 - u]
        return remote(theirs, part_in.at[q, s], x_send.at[0, s, q % DEEP], x_recv.at[0, s, q], over_first[s])

    def scatter_two(q, s):
        theirs = pair.at[q, s, 1 - second[s]]
        return remote(theirs, pair_in.at[q, s], x_send.at[1, s, q % DEEP], x_recv.at[1, s, q], over_second[s])

    def gather_one(q, s, own=True):
        b = second[s] if own else 1 - second[s]
        rows = shock.at[q + 1, c, b, v, :, wide:] if s else shock.at[q + 1, c, u, b, :, :wide]
        return remote(rows, rows, x_send.at[2, s, q % DEEP], x_recv.at[2, s, q], over_second[s])

    def gather_two(q, s, own=True):
        b = first[s] if own else 1 - first[s]
        rows = shock.at[q + 1, c, :, b, :, wide:] if s else shock.at[q + 1, c, b, :, :, :wide]
        return remote(rows, rows, x_send.at[3, s, q % DEEP], x_recv.at[3, s, q], over_first[s])

    def give_sibling(q, own=True):
        rows = shock.at[q + 1, c if own else 1 - c]
        return remote(rows, rows, sib_send.at[q % DEEP], sib_recv.at[q], sibling)

    def pass_loss(r, h, j):
        return remote(
            loss.at[r, h, (place[h][0] + j) % 4], loss_in.at[r, h, j - 1],
            f_send.at[0, h, j - 1, r % DEEP], f_recv.at[0, h, j - 1, r], over_place[h][0][j - 1],
        )

    def pass_row(r, h, j):
        return remote(
            row.at[r, h, (place[h][1] + j) % 4], row_in.at[r, h, j - 1],
            f_send.at[1, h, j - 1, r % DEEP], f_recv.at[1, h, j - 1, r], over_place[h][1][j - 1],
        )

    def launch(copy, q, *which):
        @pl.when(q >= DEEP)
        def _():
            copy(q - DEEP, *which).wait_send()

        copy(q, *which).start()

    def stage(turn, count, body):
        @pl.when((turn >= 0) & (turn < count))
        def _():
            body(turn)

    def sum_days(q):
        whole = days[...].reshape(chip_days, width)
        both = counts[pl.ds(q, 2)].reshape(2 * half, chip_days)
        total = jnp.dot(both, whole, preferred_element_type=jnp.float32).astype(part.dtype)
        for i in range(2):
            for s in range(2):
                own = total[i * half : i * half + half, s * wide : s * wide + wide]
                part[q + i, s] = own.reshape(part.shape[2:])
        for i in range(2):
            for s in range(2):
                launch(scatter_one, q + i, s)

    def sum_pairs(q):
        for s in range(2):
            scatter_one(q, s).wait_recv()
            kept = part[q, 1, :, v] if s else part[q, 0, u]
            total = kept.astype(jnp.float32) + part_in[q, s].astype(jnp.float32)
            pair[q, s] = total.astype(pair.dtype)
            launch(scatter_two, q, s)

    def sum_chips(q):
        for s in range(2):
            scatter_two(q, s).wait_recv()
            total = pair[q, s, second[s]].astype(jnp.float32) + pair_in[q, s].astype(jnp.float32)
            scaled = total * -vol[:, s * wide : s * wide + wide]
            shock[q + 1, c, u, v, :, s * wide : s * wide + wide] = scaled.astype(shock.dtype)
            launch(gather_one, q, s)

    def spread(q):
        for s in range(2):
            gather_one(q, s, False).wait_recv()
            launch(gather_two, q, s)

    def cross(q):
        for s in range(2):
            gather_two(q, s, False).wait_recv()
        launch(give_sibling, q)

    def revalue(r):
        @pl.when(r == 0)
        def _():
            load_book.wait()

        @pl.when(r > 0)
        def _():
            give_sibling(r - 1, False).wait_recv()

        moves = shock[r].reshape(2 * half, width)
        value = lax.dot_general(
            book[...], moves, (((1,), (1,)), ((), ())), preferred_element_type=jnp.float32
        ).astype(loss.dtype)
        few = mine // 2
        for h in range(2):
            for owner in range(16):
                at = (owner // 4, owner % 4) if h else (owner % 4, owner // 4)
                top = owner * mine + h * few
                loss[r, h, at[0], at[1]] = value[top : top + few]
        for h in range(2):
            for j in range(1, 4):
                launch(pass_loss, r, h, j)

    def fold(r):
        for h in range(2):
            total = loss[r, h, place[h][0]].astype(jnp.float32)
            for j in range(1, 4):
                pass_loss(r, h, j).wait_recv()
                total = total + loss_in[r, h, j - 1].astype(jnp.float32)
            row[r, h] = total.astype(row.dtype)
            for j in range(1, 4):
                launch(pass_row, r, h, j)

    def finish(r):
        few = mine // 2
        for h in range(2):
            total = row[r, h, place[h][1]].astype(jnp.float32)
            for j in range(1, 4):
                pass_row(r, h, j).wait_recv()
                total = total + row_in[r, h, j - 1].astype(jnp.float32)

            @pl.when(r > 0)
            def _():
                at = pl.multiple_of((r - 1) * 2 * half, 2 * half)
                out[h * few : h * few + few, pl.ds(at, 2 * half)] = total.astype(out.dtype)
                sums[h * few : h * few + few, :] = sums[h * few : h * few + few, :] + jnp.exp(total)

            @pl.when(r == 0)
            def _():
                owed[h * few : h * few + few, :] = total

    def turn(t, carry):
        stage(t - PAIRS, CHUNKS, sum_pairs)
        stage(t - CHIPS, CHUNKS, sum_chips)
        stage(t - SPREAD, CHUNKS, spread)
        stage(t - CROSS, CHUNKS, cross)
        stage(jnp.where(t % 2 == 0, t, -1), CHUNKS, sum_days)
        stage(t + 2, CHUNKS, count_days)
        stage(t - REVALUE, CHUNKS + 1, revalue)
        stage(t - FOLD, CHUNKS + 1, fold)
        stage(t - FINISH, CHUNKS + 1, finish)
        return carry

    lax.fori_loop(0, CHUNKS + 1 + FINISH, turn, 0)

    level = jnp.log(jnp.sum(sums[...], axis=1, keepdims=True) * (1.0 / paths))
    diagonal = lax.broadcasted_iota(jnp.int32, (mine, mine), 0) == lax.broadcasted_iota(
        jnp.int32, (mine, mine), 1
    )
    margin[...] = jnp.sum(jnp.where(diagonal, level, 0.0), axis=0, keepdims=True)
    over = owed[:, 0:1] - level
    shortfall[...] = jnp.sum(jnp.where(diagonal, over, 0.0), axis=0, keepdims=True)

    def sent(i, carry):
        for h in range(2):
            for j in range(1, 4):
                pass_loss(CHUNKS - i, h, j).wait_send()
                pass_row(CHUNKS - i, h, j).wait_send()
        for s in range(2):
            for copy in (scatter_one, scatter_two, gather_one, gather_two):
                copy(CHUNKS - 1 - i, s).wait_send()
        give_sibling(CHUNKS - 1 - i).wait_send()
        return carry

    lax.fori_loop(0, DEEP, sent, 0)


def hand_over(*refs):
    for array, result in zip(refs[:3], refs[3:]):
        result[...] = array[...]


def local(history, block_starts, block_lengths, vol_scale, exposure, realized):
    own_days, width = history.shape
    paths = block_starts.shape[0]
    accounts = exposure.shape[0]
    mine = accounts // 16
    q, r = CHUNKS, CHUNKS + 1
    half = paths // q // 2
    block, wide, few = half // 4, width // 2, mine // 2
    vmem = pl.BlockSpec(memory_space=pltpu.VMEM)
    raw = pl.BlockSpec(memory_space=pl.ANY)
    bf16, f32 = jnp.bfloat16, jnp.float32
    dma = pltpu.SemaphoreType.DMA
    results = (
        jax.ShapeDtypeStruct((mine, paths), bf16),
        jax.ShapeDtypeStruct((1, mine), f32),
        jax.ShapeDtypeStruct((1, mine), f32),
    )
    found = pl.pallas_call(
        kernel,
        out_shape=results,
        in_specs=[raw, vmem, vmem, vmem, raw, vmem],
        out_specs=(vmem, vmem, vmem),
        scratch_shapes=[
            pltpu.VMEM((2, own_days, width), bf16),
            pltpu.VMEM((accounts, width), bf16),
            pltpu.VMEM((128, 128), f32),
            pltpu.VMEM((q, half, 2 * own_days), bf16),
            pltpu.VMEM((q, 2, 2, 2, block, wide), bf16),
            pltpu.VMEM((q, 2, 2, block, wide), bf16),
            pltpu.VMEM((q, 2, 2, block, wide), bf16),
            pltpu.VMEM((q, 2, block, wide), bf16),
            pltpu.VMEM((r, 2, 2, 2, block, width), bf16),
            pltpu.VMEM((r, 2, 4, 4, few, 2 * half), bf16),
            pltpu.VMEM((r, 2, 3, 4, few, 2 * half), bf16),
            pltpu.VMEM((r, 2, 4, few, 2 * half), bf16),
            pltpu.VMEM((r, 2, 3, few, 2 * half), bf16),
            pltpu.VMEM((mine, 2 * half), f32),
            pltpu.VMEM((mine, 2 * half), f32),
            dma((2,)),
            dma,
            dma,
            dma((4, 2, DEEP)),
            dma((4, 2, q)),
            dma((DEEP,)),
            dma((q,)),
            dma((2, 2, 3, DEEP)),
            dma((2, 2, 3, r)),
        ],
        compiler_params=pltpu.CompilerParams(
            collective_id=0, has_side_effects=True, vmem_limit_bytes=60 << 20
        ),
        name="backtest",
    )(history, block_starts.T, block_lengths.T, vol_scale.reshape(1, width), exposure, realized)
    out, margin, shortfall = pl.pallas_call(
        hand_over,
        out_shape=results,
        in_specs=[vmem] * 3,
        out_specs=(vmem,) * 3,
        name="results",
    )(*found)
    return out, margin.reshape(mine), shortfall.reshape(mine)


def solution(mesh):
    in_specs = (P("days", "fac"), P(), P(), P("fac"), P("days", "fac"), P("fac"))
    out_specs = (P(("days", "fac"), None), P(("days", "fac")), P(("days", "fac")))
    return jax.shard_map(local, mesh=mesh, in_specs=in_specs, out_specs=out_specs, check_vma=False)
```

time: 75.2 us -> 72.7 us (0.967)
  Pallas kernels: 74.4 us -> 71.8 us
    pallas_call x1, Pallas kernels: 72.7 us -> 70.2 us  [local(): pl.pallas_call(kernel, out_shape=results, in_specs=[raw, vmem, vmem, vmem...]
where the time goes in v3:
time: 72.7 us; the launch traced here: 72.5 us
  Pallas kernels  71.8 us (99%)
    pallas_call x1, Pallas kernels, local(): pl.pallas_call(kernel, out_shape=results, in_specs=[raw, vmem, vmem, vmem...  70.2 us
    pallas_call x1, Pallas kernels, local(): pl.pallas_call(hand_over, out_shape=results, in_specs=[vmem] * 3, out_spe...  1.68 us

profile of v3, /device:TPU:0, one launch (start us, length us, event | category | flops | bytes accessed | tf_op | source)
XLA Modules:
  0.0 72.5 jit_solution(13596864075579214106)
XLA Ops:
  0.6 70.2 %backtest.1 = (bf16[64,2048]{1,0:T(8,128)(2,1)}, f32[1,64]{1,0:T(1,128)}, f32[1,64]{1,0:T(1,128)}) custom-call(bf16[512,1024]{1,0:T(8,128)(2,1)} %hist.1, s32[4,2048]{1,0:T(4,128)} %bitcast.5, s32[4,2048]{1,0:T(4,128)} %bitcast.6, f32[1,1024]{1,0:T(1,128)} %bitcast.7, bf16[1024,1024]{1,0:T(8,128)(2,1)} %expo.1, bf16[1024]{0:T(1024)(128)(2,1)} %real.1), custom_call_target="tpu_custom_call" | custom-call | tf_op jit(solution)/shard_map/backtest/pallas_call | solution.py:292
  70.8 1.7 %results.1 = (bf16[64,2048]{1,0:T(8,128)(2,1)}, f32[1,64]{1,0:T(1,128)}, f32[1,64]{1,0:T(1,128)}) custom-call(bf16[64,2048]{1,0:T(8,128)(2,1)} %get-tuple-element.9.refs_0_, f32[1,64]{1,0:T(1,128)} %get-tuple-element.10.refs_1_, f32[1,64]{1,0:T(1,128)} %get-tuple-element.11.refs_2_), custom_call_target="tpu_custom_call" | custom-call | tf_op jit(solution)/shard_map/results/pallas_call | solution.py:328

commit v4 on v3

--- a/solution.py
+++ b/solution.py
@@ -9,7 +9,7 @@
 
 CHUNKS = 16
 PAIRS, CHIPS, SPREAD, CROSS, REVALUE, FOLD, FINISH = 3, 5, 7, 9, 9, 12, 14
-DEEP = 4
+DEEP = 2
 
 
 def bits(place):
@@ -98,21 +98,21 @@
 
     def scatter_one(q, s):
         theirs = part.at[q, 1, :, 1 - v] if s else part.at[q, 0, 1 - u]
-        return remote(theirs, part_in.at[q, s], x_send.at[0, s, q % DEEP], x_recv.at[0, s, q], over_first[s])
+        return remote(theirs, part_in.at[q, s], x_send.at[0, q % DEEP], x_recv.at[0, q], over_first[s])
 
     def scatter_two(q, s):
         theirs = pair.at[q, s, 1 - second[s]]
-        return remote(theirs, pair_in.at[q, s], x_send.at[1, s, q % DEEP], x_recv.at[1, s, q], over_second[s])
-
-    def gather_one(q, s, own=True):
-        b = second[s] if own else 1 - second[s]
+        return remote(theirs, pair_in.at[q, s], x_send.at[1, q % DEEP], x_recv.at[1, q], over_second[s])
+
+    def gather_one(q, s):
+        b = second[s]
         rows = shock.at[q + 1, c, b, v, :, wide:] if s else shock.at[q + 1, c, u, b, :, :wide]
-        return remote(rows, rows, x_send.at[2, s, q % DEEP], x_recv.at[2, s, q], over_second[s])
-
-    def gather_two(q, s, own=True):
-        b = first[s] if own else 1 - first[s]
+        return remote(rows, rows, x_send.at[2, q % DEEP], x_recv.at[2, q], over_second[s])
+
+    def gather_two(q, s):
+        b = first[s]
         rows = shock.at[q + 1, c, :, b, :, wide:] if s else shock.at[q + 1, c, b, :, :, :wide]
-        return remote(rows, rows, x_send.at[3, s, q % DEEP], x_recv.at[3, s, q], over_first[s])
+        return remote(rows, rows, x_send.at[3, q % DEEP], x_recv.at[3, q], over_first[s])
 
     def give_sibling(q, own=True):
         rows = shock.at[q + 1, c if own else 1 - c]
@@ -121,21 +121,39 @@
     def pass_loss(r, h, j):
         return remote(
             loss.at[r, h, (place[h][0] + j) % 4], loss_in.at[r, h, j - 1],
-            f_send.at[0, h, j - 1, r % DEEP], f_recv.at[0, h, j - 1, r], over_place[h][0][j - 1],
+            f_send.at[0, r % DEEP], f_recv.at[0, r], over_place[h][0][j - 1],
         )
 
     def pass_row(r, h, j):
         return remote(
             row.at[r, h, (place[h][1] + j) % 4], row_in.at[r, h, j - 1],
-            f_send.at[1, h, j - 1, r % DEEP], f_recv.at[1, h, j - 1, r], over_place[h][1][j - 1],
+            f_send.at[1, r % DEEP], f_recv.at[1, r], over_place[h][1][j - 1],
         )
 
-    def launch(copy, q, *which):
+    def x_copies(kind, q):
+        held = part_in.at[q] if kind in (0, 3) else pair_in.at[q]
+        return remote(held, held, x_send.at[kind, q % DEEP], x_recv.at[kind, q], over_u)
+
+    def f_copies(kind, r):
+        held = row_in.at[r] if kind else loss_in.at[r]
+        return remote(held, held, f_send.at[kind, r % DEEP], f_recv.at[kind, r], over_z[0])
+
+    def x_launch(kind, copy, q):
         @pl.when(q >= DEEP)
         def _():
-            copy(q - DEEP, *which).wait_send()
-
-        copy(q, *which).start()
+            x_copies(kind, q - DEEP).wait_send()
+
+        for s in range(2):
+            copy(q, s).start()
+
+    def f_launch(kind, copy, r):
+        @pl.when(r >= DEEP)
+        def _():
+            f_copies(kind, r - DEEP).wait_send()
+
+        for h in range(2):
+            for j in range(1, 4):
+                copy(r, h, j).start()
 
     def stage(turn, count, body):
         @pl.when((turn >= 0) & (turn < count))
@@ -151,34 +169,36 @@
                 own = total[i * half : i * half + half, s * wide : s * wide + wide]
                 part[q + i, s] = own.reshape(part.shape[2:])
         for i in range(2):
-            for s in range(2):
-                launch(scatter_one, q + i, s)
+            x_launch(0, scatter_one, q + i)
 
     def sum_pairs(q):
+        x_copies(0, q).wait_recv()
         for s in range(2):
-            scatter_one(q, s).wait_recv()
             kept = part[q, 1, :, v] if s else part[q, 0, u]
             total = kept.astype(jnp.float32) + part_in[q, s].astype(jnp.float32)
             pair[q, s] = total.astype(pair.dtype)
-            launch(scatter_two, q, s)
+        x_launch(1, scatter_two, q)
 
     def sum_chips(q):
+        x_copies(1, q).wait_recv()
         for s in range(2):
-            scatter_two(q, s).wait_recv()
             total = pair[q, s, second[s]].astype(jnp.float32) + pair_in[q, s].astype(jnp.float32)
             scaled = total * -vol[:, s * wide : s * wide + wide]
             shock[q + 1, c, u, v, :, s * wide : s * wide + wide] = scaled.astype(shock.dtype)
-            launch(gather_one, q, s)
+        x_launch(2, gather_one, q)
 
     def spread(q):
-        for s in range(2):
-            gather_one(q, s, False).wait_recv()
-            launch(gather_two, q, s)
+        x_copies(2, q).wait_recv()
+        x_launch(3, gather_two, q)
 
     def cross(q):
-        for s in range(2):
-            gather_two(q, s, False).wait_recv()
-        launch(give_sibling, q)
+        x_copies(3, q).wait_recv()
+
+        @pl.when(q >= DEEP)
+        def _():
+            give_sibling(q - DEEP).wait_send()
+
+        give_sibling(q).start()
 
     def revalue(r):
         @pl.when(r == 0)
@@ -199,26 +219,23 @@
                 at = (owner // 4, owner % 4) if h else (owner % 4, owner // 4)
                 top = owner * mine + h * few
                 loss[r, h, at[0], at[1]] = value[top : top + few]
-        for h in range(2):
-            for j in range(1, 4):
-                launch(pass_loss, r, h, j)
+        f_launch(0, pass_loss, r)
 
     def fold(r):
+        f_copies(0, r).wait_recv()
         for h in range(2):
             total = loss[r, h, place[h][0]].astype(jnp.float32)
             for j in range(1, 4):
-                pass_loss(r, h, j).wait_recv()
                 total = total + loss_in[r, h, j - 1].astype(jnp.float32)
             row[r, h] = total.astype(row.dtype)
-            for j in range(1, 4):
-                launch(pass_row, r, h, j)
+        f_launch(1, pass_row, r)
 
     def finish(r):
         few = mine // 2
+        f_copies(1, r).wait_recv()
         for h in range(2):
             total = row[r, h, place[h][1]].astype(jnp.float32)
             for j in range(1, 4):
-                pass_row(r, h, j).wait_recv()
                 total = total + row_in[r, h, j - 1].astype(jnp.float32)
 
             @pl.when(r > 0)
@@ -254,13 +271,10 @@
     shortfall[...] = jnp.sum(jnp.where(diagonal, over, 0.0), axis=0, keepdims=True)
 
     def sent(i, carry):
-        for h in range(2):
-            for j in range(1, 4):
-                pass_loss(CHUNKS - i, h, j).wait_send()
-                pass_row(CHUNKS - i, h, j).wait_send()
-        for s in range(2):
-            for copy in (scatter_one, scatter_two, gather_one, gather_two):
-                copy(CHUNKS - 1 - i, s).wait_send()
+        for kind in range(2):
+            f_copies(kind, CHUNKS - i).wait_send()
+        for kind in range(4):
+            x_copies(kind, CHUNKS - 1 - i).wait_send()
         give_sibling(CHUNKS - 1 - i).wait_send()
         return carry
 
@@ -313,12 +327,12 @@
             dma((2,)),
             dma,
             dma,
-            dma((4, 2, DEEP)),
-            dma((4, 2, q)),
+            dma((4, DEEP)),
+            dma((4, q)),
             dma((DEEP,)),
             dma((q,)),
-            dma((2, 2, 3, DEEP)),
-            dma((2, 2, 3, r)),
+            dma((2, DEEP)),
+            dma((2, r)),
         ],
         compiler_params=pltpu.CompilerParams(
             collective_id=0, has_side_effects=True, vmem_limit_bytes=60 << 20

time: 72.7 us -> 69.6 us (0.957)
  Pallas kernels: 71.8 us -> 68.8 us
    pallas_call x1, Pallas kernels: 70.2 us -> 67.1 us  [local(): pl.pallas_call(kernel, out_shape=results, in_specs=[raw, vmem, vmem, vmem...]
where the time goes in v4:
time: 69.6 us; the launch traced here: 69.4 us
  Pallas kernels  68.8 us (99%)
    pallas_call x1, Pallas kernels, local(): pl.pallas_call(kernel, out_shape=results, in_specs=[raw, vmem, vmem, vmem...  67.1 us
    pallas_call x1, Pallas kernels, local(): pl.pallas_call(hand_over, out_shape=results, in_specs=[vmem] * 3, out_spe...  1.68 us

profile of v4, /device:TPU:0, one launch (start us, length us, event | category | flops | bytes accessed | tf_op | source)
XLA Modules:
  0.0 69.4 jit_solution(10570915628199337712)
XLA Ops:
  0.6 67.1 %backtest.1 = (bf16[64,2048]{1,0:T(8,128)(2,1)}, f32[1,64]{1,0:T(1,128)}, f32[1,64]{1,0:T(1,128)}) custom-call(bf16[512,1024]{1,0:T(8,128)(2,1)} %hist.1, s32[4,2048]{1,0:T(4,128)} %bitcast.5, s32[4,2048]{1,0:T(4,128)} %bitcast.6, f32[1,1024]{1,0:T(1,128)} %bitcast.7, bf16[1024,1024]{1,0:T(8,128)(2,1)} %expo.1, bf16[1024]{0:T(1024)(128)(2,1)} %real.1), custom_call_target="tpu_custom_call" | custom-call | tf_op jit(solution)/shard_map/backtest/pallas_call | solution.py:306
  67.7 1.7 %results.1 = (bf16[64,2048]{1,0:T(8,128)(2,1)}, f32[1,64]{1,0:T(1,128)}, f32[1,64]{1,0:T(1,128)}) custom-call(bf16[64,2048]{1,0:T(8,128)(2,1)} %get-tuple-element.9.refs_0_, f32[1,64]{1,0:T(1,128)} %get-tuple-element.10.refs_1_, f32[1,64]{1,0:T(1,128)} %get-tuple-element.11.refs_2_), custom_call_target="tpu_custom_call" | custom-call | tf_op jit(solution)/shard_map/results/pallas_call | solution.py:342

commit v5 on v4

--- a/solution.py
+++ b/solution.py
@@ -10,6 +10,7 @@
 CHUNKS = 16
 PAIRS, CHIPS, SPREAD, CROSS, REVALUE, FOLD, FINISH = 3, 5, 7, 9, 9, 12, 14
 DEEP = 2
+FAR = 8
 
 
 def bits(place):
@@ -61,8 +62,14 @@
         pl.semaphore_signal(barrier, inc=1, device_id=device, device_id_type=pl.DeviceIdType.MESH)
     pl.semaphore_wait(barrier, len(everyone))
 
-    share_days = remote(hist, days.at[c], days_send, days_recv, sibling)
-    share_days.start()
+    wide = width // 2
+    share_days = []
+    for s in range(2):
+        columns = pl.ds(s * wide, wide)
+        share_days.append(
+            remote(hist.at[:, columns], days.at[c, :, columns], days_send.at[s], days_recv.at[s], sibling)
+        )
+        share_days[s].start()
 
     shock[0] = jnp.zeros(shock.shape[1:], shock.dtype)
     lead = shock.shape[4]
@@ -72,7 +79,6 @@
     sums[...] = jnp.zeros_like(sums)
 
     half = paths // CHUNKS // 2
-    wide = width // 2
     chip_days = 2 * own_days
     mine = out.shape[0]
 
@@ -94,49 +100,48 @@
     count_days(0)
     count_days(1)
     load_days.wait()
-    share_days.wait()
 
     def scatter_one(q, s):
         theirs = part.at[q, 1, :, 1 - v] if s else part.at[q, 0, 1 - u]
-        return remote(theirs, part_in.at[q, s], x_send.at[0, q % DEEP], x_recv.at[0, q], over_first[s])
+        return remote(theirs, part_in.at[q, s], x_send.at[0, q % DEEP], x_recv.at[0, q % FAR], over_first[s])
 
     def scatter_two(q, s):
         theirs = pair.at[q, s, 1 - second[s]]
-        return remote(theirs, pair_in.at[q, s], x_send.at[1, q % DEEP], x_recv.at[1, q], over_second[s])
+        return remote(theirs, pair_in.at[q, s], x_send.at[1, q % DEEP], x_recv.at[1, q % FAR], over_second[s])
 
     def gather_one(q, s):
         b = second[s]
         rows = shock.at[q + 1, c, b, v, :, wide:] if s else shock.at[q + 1, c, u, b, :, :wide]
-        return remote(rows, rows, x_send.at[2, q % DEEP], x_recv.at[2, q], over_second[s])
+        return remote(rows, rows, x_send.at[2, q % DEEP], x_recv.at[2, q % FAR], over_second[s])
 
     def gather_two(q, s):
         b = first[s]
         rows = shock.at[q + 1, c, :, b, :, wide:] if s else shock.at[q + 1, c, b, :, :, :wide]
-        return remote(rows, rows, x_send.at[3, q % DEEP], x_recv.at[3, q], over_first[s])
+        return remote(rows, rows, x_send.at[3, q % DEEP], x_recv.at[3, q % FAR], over_first[s])
 
     def give_sibling(q, own=True):
         rows = shock.at[q + 1, c if own else 1 - c]
-        return remote(rows, rows, sib_send.at[q % DEEP], sib_recv.at[q], sibling)
+        return remote(rows, rows, sib_send.at[q % DEEP], sib_recv.at[q % FAR], sibling)
 
     def pass_loss(r, h, j):
         return remote(
             loss.at[r, h, (place[h][0] + j) % 4], loss_in.at[r, h, j - 1],
-            f_send.at[0, r % DEEP], f_recv.at[0, r], over_place[h][0][j - 1],
+            f_send.at[0, r % DEEP], f_recv.at[0, r % FAR], over_place[h][0][j - 1],
         )
 
     def pass_row(r, h, j):
         return remote(
             row.at[r, h, (place[h][1] + j) % 4], row_in.at[r, h, j - 1],
-            f_send.at[1, r % DEEP], f_recv.at[1, r], over_place[h][1][j - 1],
+            f_send.at[1, r % DEEP], f_recv.at[1, r % FAR], over_place[h][1][j - 1],
         )
 
     def x_copies(kind, q):
         held = part_in.at[q] if kind in (0, 3) else pair_in.at[q]
-        return remote(held, held, x_send.at[kind, q % DEEP], x_recv.at[kind, q], over_u)
+        return remote(held, held, x_send.at[kind, q % DEEP], x_recv.at[kind, q % FAR], over_u)
 
     def f_copies(kind, r):
         held = row_in.at[r] if kind else loss_in.at[r]
-        return remote(held, held, f_send.at[kind, r % DEEP], f_recv.at[kind, r], over_z[0])
+        return remote(held, held, f_send.at[kind, r % DEEP], f_recv.at[kind, r % FAR], over_z[0])
 
     def x_launch(kind, copy, q):
         @pl.when(q >= DEEP)
@@ -151,8 +156,8 @@
         def _():
             f_copies(kind, r - DEEP).wait_send()
 
-        for h in range(2):
-            for j in range(1, 4):
+        for j in (2, 1, 3):
+            for h in range(2):
                 copy(r, h, j).start()
 
     def stage(turn, count, body):
@@ -161,15 +166,24 @@
             body(turn)
 
     def sum_days(q):
-        whole = days[...].reshape(chip_days, width)
+        @pl.when(q >= DEEP)
+        def _():
+            for i in range(2):
+                x_copies(0, q + i - DEEP).wait_send()
+
         both = counts[pl.ds(q, 2)].reshape(2 * half, chip_days)
-        total = jnp.dot(both, whole, preferred_element_type=jnp.float32).astype(part.dtype)
-        for i in range(2):
-            for s in range(2):
-                own = total[i * half : i * half + half, s * wide : s * wide + wide]
-                part[q + i, s] = own.reshape(part.shape[2:])
-        for i in range(2):
-            x_launch(0, scatter_one, q + i)
+        for s in range(2):
+
+            @pl.when(q == 0)
+            def _():
+                share_days[s].wait()
+
+            columns = slice(s * wide, s * wide + wide)
+            whole = days[:, :, columns].reshape(chip_days, wide)
+            total = jnp.dot(both, whole, preferred_element_type=jnp.float32).astype(part.dtype)
+            for i in range(2):
+                part[q + i, s] = total[i * half : i * half + half].reshape(part.shape[2:])
+                scatter_one(q + i, s).start()
 
     def sum_pairs(q):
         x_copies(0, q).wait_recv()
@@ -325,14 +339,14 @@
             pltpu.VMEM((mine, 2 * half), f32),
             pltpu.VMEM((mine, 2 * half), f32),
             dma((2,)),
-            dma,
-            dma,
+            dma((2,)),
+            dma((2,)),
             dma((4, DEEP)),
-            dma((4, q)),
+            dma((4, FAR)),
             dma((DEEP,)),
-            dma((q,)),
+            dma((FAR,)),
             dma((2, DEEP)),
-            dma((2, r)),
+            dma((2, FAR)),
         ],
         compiler_params=pltpu.CompilerParams(
             collective_id=0, has_side_effects=True, vmem_limit_bytes=60 << 20

time: 69.6 us -> 68.9 us (0.990)
  Pallas kernels: 68.8 us -> 68.1 us
where the time goes in v5:
time: 68.9 us; the launch traced here: 68.7 us
  Pallas kernels  68.1 us (99%)
    pallas_call x1, Pallas kernels, local(): pl.pallas_call(kernel, out_shape=results, in_specs=[raw, vmem, vmem, vmem...  66.4 us
    pallas_call x1, Pallas kernels, local(): pl.pallas_call(hand_over, out_shape=results, in_specs=[vmem] * 3, out_spe...  1.68 us

profile of v5, /device:TPU:0, one launch (start us, length us, event | category | flops | bytes accessed | tf_op | source)
XLA Modules:
  0.0 68.7 jit_solution(10602969107484301682)
XLA Ops:
  0.6 66.4 %backtest.1 = (bf16[64,2048]{1,0:T(8,128)(2,1)}, f32[1,64]{1,0:T(1,128)}, f32[1,64]{1,0:T(1,128)}) custom-call(bf16[512,1024]{1,0:T(8,128)(2,1)} %hist.1, s32[4,2048]{1,0:T(4,128)} %bitcast.5, s32[4,2048]{1,0:T(4,128)} %bitcast.6, f32[1,1024]{1,0:T(1,128)} %bitcast.7, bf16[1024,1024]{1,0:T(8,128)(2,1)} %expo.1, bf16[1024]{0:T(1024)(128)(2,1)} %real.1), custom_call_target="tpu_custom_call" | custom-call | tf_op jit(solution)/shard_map/backtest/pallas_call | solution.py:320
  67.1 1.7 %results.1 = (bf16[64,2048]{1,0:T(8,128)(2,1)}, f32[1,64]{1,0:T(1,128)}, f32[1,64]{1,0:T(1,128)}) custom-call(bf16[64,2048]{1,0:T(8,128)(2,1)} %get-tuple-element.9.refs_0_, f32[1,64]{1,0:T(1,128)} %get-tuple-element.10.refs_1_, f32[1,64]{1,0:T(1,128)} %get-tuple-element.11.refs_2_), custom_call_target="tpu_custom_call" | custom-call | tf_op jit(solution)/shard_map/results/pallas_call | solution.py:356

commit v6 on v5

--- a/solution.py
+++ b/solution.py
@@ -32,8 +32,8 @@
     hist, starts, lens, vol, expo, real,
     out, margin, shortfall,
     days, book, table, counts, part, part_in, pair, pair_in, shock,
-    loss, loss_in, row, row_in, sums, owed,
-    here, days_send, days_recv, x_send, x_recv, sib_send, sib_recv, f_send, f_recv,
+    loss, loss_in, row, row_in, sums, owed, held,
+    here, leave, days_send, days_recv, x_send, x_recv, sib_send, sib_recv, f_send, f_recv,
 ):
     own_days, width = hist.shape
     paths = starts.shape[1]
@@ -255,12 +255,17 @@
             @pl.when(r > 0)
             def _():
                 at = pl.multiple_of((r - 1) * 2 * half, 2 * half)
-                out[h * few : h * few + few, pl.ds(at, 2 * half)] = total.astype(out.dtype)
+                held[h * few : h * few + few, pl.ds(at, 2 * half)] = total.astype(out.dtype)
                 sums[h * few : h * few + few, :] = sums[h * few : h * few + few, :] + jnp.exp(total)
 
             @pl.when(r == 0)
             def _():
                 owed[h * few : h * few + few, :] = total
+
+        @pl.when(r > 0)
+        def _():
+            lanes = pl.ds(pl.multiple_of((r - 1) * 2 * half, 2 * half), 2 * half)
+            pltpu.make_async_copy(held.at[:, lanes], out.at[:, lanes], leave).start()
 
     def turn(t, carry):
         stage(t - PAIRS, CHUNKS, sum_pairs)
@@ -293,6 +298,7 @@
         return carry
 
     lax.fori_loop(0, DEEP, sent, 0)
+    pltpu.make_async_copy(held, out, leave).wait()
 
 
 def hand_over(*refs):
@@ -321,7 +327,7 @@
         kernel,
         out_shape=results,
         in_specs=[raw, vmem, vmem, vmem, raw, vmem],
-        out_specs=(vmem, vmem, vmem),
+        out_specs=(raw, vmem, vmem),
         scratch_shapes=[
             pltpu.VMEM((2, own_days, width), bf16),
             pltpu.VMEM((accounts, width), bf16),
@@ -338,7 +344,9 @@
             pltpu.VMEM((r, 2, 3, few, 2 * half), bf16),
             pltpu.VMEM((mine, 2 * half), f32),
             pltpu.VMEM((mine, 2 * half), f32),
+            pltpu.VMEM((mine, paths), bf16),
             dma((2,)),
+            dma,
             dma((2,)),
             dma((2,)),
             dma((4, DEEP)),

time: 68.9 us -> 69.2 us (level)
  no operation moved by 1% of the time
where the time goes in v6:
time: 69.2 us; the launch traced here: 69 us
  Pallas kernels  68.4 us (99%)
    pallas_call x1, Pallas kernels, local(): pl.pallas_call(kernel, out_shape=results, in_specs=[raw, vmem, vmem, vmem...  66.7 us
    pallas_call x1, Pallas kernels, local(): pl.pallas_call(hand_over, out_shape=results, in_specs=[vmem] * 3, out_spe...  1.68 us

profile of v6, /device:TPU:0, one launch (start us, length us, event | category | flops | bytes accessed | tf_op | source)
XLA Modules:
  0.0 69.0 jit_solution(14905752481508122305)
XLA Ops:
  0.6 66.7 %backtest.1 = (bf16[64,2048]{1,0:T(8,128)(2,1)}, f32[1,64]{1,0:T(1,128)}, f32[1,64]{1,0:T(1,128)}) custom-call(bf16[512,1024]{1,0:T(8,128)(2,1)} %hist.1, s32[4,2048]{1,0:T(4,128)} %bitcast.5, s32[4,2048]{1,0:T(4,128)} %bitcast.6, f32[1,1024]{1,0:T(1,128)} %bitcast.7, bf16[1024,1024]{1,0:T(8,128)(2,1)} %expo.1, bf16[1024]{0:T(1024)(128)(2,1)} %real.1), custom_call_target="tpu_custom_call" | custom-call | tf_op jit(solution)/shard_map/backtest/pallas_call | solution.py:326
  67.3 1.7 %results.1 = (bf16[64,2048]{1,0:T(8,128)(2,1)}, f32[1,64]{1,0:T(1,128)}, f32[1,64]{1,0:T(1,128)}) custom-call(bf16[64,2048]{1,0:T(8,128)(2,1)} %get-tuple-element.9.refs_0_, f32[1,64]{1,0:T(1,128)} %get-tuple-element.10.refs_1_, f32[1,64]{1,0:T(1,128)} %get-tuple-element.11.refs_2_), custom_call_target="tpu_custom_call" | custom-call | tf_op jit(solution)/shard_map/results/pallas_call | solution.py:364

commit v7 on v5

--- a/solution.py
+++ b/solution.py
@@ -189,8 +189,7 @@
         x_copies(0, q).wait_recv()
         for s in range(2):
             kept = part[q, 1, :, v] if s else part[q, 0, u]
-            total = kept.astype(jnp.float32) + part_in[q, s].astype(jnp.float32)
-            pair[q, s] = total.astype(pair.dtype)
+            pair[q, s] = kept + part_in[q, s]
         x_launch(1, scatter_two, q)
 
     def sum_chips(q):

time: 68.9 us -> 69.1 us (level)
  no operation moved by 1% of the time
where the time goes in v7:
time: 69.1 us; the launch traced here: 68.9 us
  Pallas kernels  68.2 us (99%)
    pallas_call x1, Pallas kernels, local(): pl.pallas_call(kernel, out_shape=results, in_specs=[raw, vmem, vmem, vmem...  66.5 us
    pallas_call x1, Pallas kernels, local(): pl.pallas_call(hand_over, out_shape=results, in_specs=[vmem] * 3, out_spe...  1.68 us

profile of v7, /device:TPU:0, one launch (start us, length us, event | category | flops | bytes accessed | tf_op | source)
XLA Modules:
  0.0 68.9 jit_solution(4845592059795408091)
XLA Ops:
  0.6 66.5 %backtest.1 = (bf16[64,2048]{1,0:T(8,128)(2,1)}, f32[1,64]{1,0:T(1,128)}, f32[1,64]{1,0:T(1,128)}) custom-call(bf16[512,1024]{1,0:T(8,128)(2,1)} %hist.1, s32[4,2048]{1,0:T(4,128)} %bitcast.5, s32[4,2048]{1,0:T(4,128)} %bitcast.6, f32[1,1024]{1,0:T(1,128)} %bitcast.7, bf16[1024,1024]{1,0:T(8,128)(2,1)} %expo.1, bf16[1024]{0:T(1024)(128)(2,1)} %real.1), custom_call_target="tpu_custom_call" | custom-call | tf_op jit(solution)/shard_map/backtest/pallas_call | solution.py:319
  67.2 1.7 %results.1 = (bf16[64,2048]{1,0:T(8,128)(2,1)}, f32[1,64]{1,0:T(1,128)}, f32[1,64]{1,0:T(1,128)}) custom-call(bf16[64,2048]{1,0:T(8,128)(2,1)} %get-tuple-element.9.refs_0_, f32[1,64]{1,0:T(1,128)} %get-tuple-element.10.refs_1_, f32[1,64]{1,0:T(1,128)} %get-tuple-element.11.refs_2_), custom_call_target="tpu_custom_call" | custom-call | tf_op jit(solution)/shard_map/results/pallas_call | solution.py:355
